TPU v7x, 32 devices: a whole 2x2x4 slice. The times are simulated.
32 devices in a mesh: dp: 8 (over y, x, core), tensor: 4 (over z).
Axes of the slice: x: 2, y: 2, z: 4, core: 2. Of those that a mesh axis runs over, the one named last changes fastest.
Arguments:
- tokens: bfloat16 [16384, 2048], P(('dp', 'tensor'))
- teacher: bfloat16 [16384, 2048], P(('dp', 'tensor')), may hold values from -6 to 6
- valid: int32 [16384], P(('dp', 'tensor')), may hold values from 0 to 1, as said below
- prefix: int32 [16], P('dp'), may hold values from 102 to 512, as said below
- w_query: bfloat16 [2048, 1024], P(None, 'tensor'), may hold values from -0.125 to 0.125
- key_weight: bfloat16 [2048, 256], replicated, may hold values from -0.125 to 0.125
- value_weight: bfloat16 [2048, 256], replicated, may hold values from -0.125 to 0.125
- query_gain: float32 [64], replicated, may hold values from 0.25 to 1.75
- key_gain: float32 [64], replicated, may hold values from 0.25 to 1.75
- w_out: bfloat16 [1024, 2048], P('tensor'), may hold values from -3 to 3
- attn_gain: float32 [2048], replicated, may hold values from 0.25 to 1.75
- ffn_gain: float32 [2048], replicated, may hold values from 0.25 to 1.75
- w_gate: bfloat16 [2048, 5120], P(None, 'tensor'), may hold values from -0.125 to 0.125
- w_up: bfloat16 [2048, 5120], P(None, 'tensor'), may hold values from -0.125 to 0.125
- w_down: bfloat16 [5120, 2048], P('tensor'), may hold values from -0.078125 to 0.078125
Outputs:
- output: bfloat16 [16384, 2048], P(('dp', 'tensor'))
- loss: float32 [], replicated
- grad_tokens: float32 [16384, 2048], P(('dp', 'tensor'))
- grad_query: float32 [2048, 1024], P(None, 'tensor')
- grad_key: float32 [2048, 256], replicated
- grad_value: float32 [2048, 256], replicated
- grad_query_gain: float32 [64], replicated
- grad_key_gain: float32 [64], replicated
- grad_out: float32 [1024, 2048], P('tensor')
- grad_attn_gain: float32 [2048], replicated
- grad_ffn_gain: float32 [2048], replicated
- grad_gate: float32 [2048, 5120], P(None, 'tensor')
- grad_up: float32 [2048, 5120], P(None, 'tensor')
- grad_down: float32 [5120, 2048], P('tensor')
Inputs may be any that keep to these rules, and one draw needn't show every extreme that they name: The first token of every sequence is valid. One sequence has prefix length exactly 512 and another exactly 102.
All inputs are finite; a program needn't handle non-finite values.
Results may differ from a plain program's by a relative error of at most 0.015.
Values may be sent and summed in bfloat16 or wider, within the bound.
A program may use at most 256 MiB of HBM per device.

v0:
```python
import jax
import jax.numpy as jnp
from jax import lax
from jax.sharding import PartitionSpec as P

QUERY_HEADS = 16
KEY_VALUE_HEADS = 4
HEAD_SIZE = 64
SEQ_LEN = 1024
EPSILON = 1e-06


def rope_tables(sequence_length, head_size):
    half_size = head_size // 2
    frequency = 10000.0 ** (-2.0 * jnp.arange(half_size, dtype=jnp.float32) / head_size)
    angles = jnp.arange(sequence_length, dtype=jnp.float32)[:, None] * frequency[None, :]
    cosine = jnp.concatenate([jnp.cos(angles), jnp.cos(angles)], 1)
    sine_tab = jnp.concatenate([jnp.sin(angles), jnp.sin(angles)], 1)
    return (cosine, sine_tab)


def rotate(vector, cosine, sine_tab):
    half_size = vector.shape[-1] // 2
    turned = jnp.concatenate([-vector[..., half_size:], vector[..., :half_size]], -1)
    return vector * cosine + turned * sine_tab


def unrotate(gradient, cosine, sine_tab):
    half_size = gradient.shape[-1] // 2
    shifted = gradient * sine_tab
    return gradient * cosine + jnp.concatenate(
        [shifted[..., half_size:], -shifted[..., :half_size]], -1
    )


def inv_root(vector):
    return lax.rsqrt(jnp.mean(vector * vector, axis=-1, keepdims=True) + EPSILON)


def norm_back(gradient, source, factor, gain_vec):
    scaled = gradient * gain_vec
    return factor * scaled - source * factor**3 * jnp.mean(scaled * source, axis=-1, keepdims=True)


def visible(sequence_length, prefix_len):
    row_pos = jnp.arange(sequence_length)[:, None]
    col_pos = jnp.arange(sequence_length)[None, :]
    return (col_pos <= row_pos) | (row_pos < prefix_len) & (col_pos < prefix_len)


def attend(query_matrix, key_matrix, value_matrix, prefix_len, kv_dev):
    sequence_length, head_count, head_size = query_matrix.shape
    grouped_heads = query_matrix.reshape(sequence_length, kv_dev, head_count // kv_dev, head_size)
    scores = jnp.einsum(
        "ikgd,jkd->kgij", grouped_heads, key_matrix, preferred_element_type=jnp.float32
    ) * head_size ** (-0.5)
    allowed = visible(sequence_length, prefix_len)
    scores = jnp.where(allowed, scores, -1e30)
    row_max = jnp.max(scores, -1, keepdims=True)
    weights = jnp.where(allowed, jnp.exp(scores - row_max), 0.0)
    row_total = jnp.sum(weights, -1, keepdims=True)
    attn_probs = (weights / row_total).astype(jnp.bfloat16)
    attended = jnp.einsum(
        "kgij,jkd->ikgd", attn_probs, value_matrix, preferred_element_type=jnp.float32
    )
    return (
        attended.reshape(sequence_length, head_count * head_size),
        (row_max + jnp.log(row_total))[..., 0],
    )


def attend_back(query_matrix, key_matrix, value_matrix, prefix_len, summit, grad_attended, kv_dev):
    sequence_length, head_count, head_size = query_matrix.shape
    per_group = head_count // kv_dev
    score_scale = head_size ** (-0.5)
    grouped_heads = query_matrix.reshape(sequence_length, kv_dev, per_group, head_size)
    scores = (
        jnp.einsum("ikgd,jkd->kgij", grouped_heads, key_matrix, preferred_element_type=jnp.float32)
        * score_scale
    )
    allowed = visible(sequence_length, prefix_len)
    attn_probs = jnp.where(
        allowed, jnp.exp(jnp.where(allowed, scores, -1e30) - summit[..., None]), 0.0
    )
    grad_heads = grad_attended.reshape(sequence_length, kv_dev, per_group, head_size)
    grad_probs = jnp.einsum(
        "ikgd,jkd->kgij", grad_heads, value_matrix, preferred_element_type=jnp.float32
    )
    inner_sum = jnp.sum(attn_probs * grad_probs, -1, keepdims=True)
    grad_scores = (attn_probs * (grad_probs - inner_sum)).astype(jnp.bfloat16)
    grad_query = (
        jnp.einsum("kgij,jkd->ikgd", grad_scores, key_matrix, preferred_element_type=jnp.float32)
        * score_scale
    )
    grad_key = (
        jnp.einsum("kgij,ikgd->jkd", grad_scores, grouped_heads, preferred_element_type=jnp.float32)
        * score_scale
    )
    grad_value = jnp.einsum(
        "kgij,ikgd->jkd",
        attn_probs.astype(jnp.bfloat16),
        grad_heads,
        preferred_element_type=jnp.float32,
    )
    return (grad_query.reshape(sequence_length, head_count, head_size), grad_key, grad_value)


def body(
    tokens,
    teacher,
    valid,
    prefix,
    w_query,
    key_weight,
    value_weight,
    query_gain,
    key_gain,
    w_out,
    attn_gain,
    ffn_gain,
    w_gate,
    w_up,
    w_down,
):
    rows_dev, width = tokens.shape
    seq_count = prefix.shape[0]
    sequence_length = SEQ_LEN
    group_rows = seq_count * sequence_length
    heads_dev = w_query.shape[1] // HEAD_SIZE
    queries_per_group = QUERY_HEADS // KEY_VALUE_HEADS
    kv_dev = max(1, heads_dev // queries_per_group)
    query_cols = heads_dev * HEAD_SIZE
    kv_cols = kv_dev * HEAD_SIZE
    kv_start = lax.axis_index("tensor") * heads_dev // queries_per_group * HEAD_SIZE
    key_local = lax.dynamic_slice_in_dim(key_weight, kv_start, kv_cols, 1)
    value_local = lax.dynamic_slice_in_dim(value_weight, kv_start, kv_cols, 1)
    source = tokens.astype(jnp.float32)
    factor_one = inv_root(source)
    normed_input = (source * factor_one * attn_gain).astype(jnp.bfloat16)
    normed_all = lax.all_gather(normed_input, "tensor", axis=0, tiled=True)
    proj_weight = jnp.concatenate([w_query, key_local, value_local], 1)
    projected = jnp.dot(normed_all, proj_weight, preferred_element_type=jnp.float32)
    query_raw = projected[:, :query_cols].reshape(group_rows, heads_dev, HEAD_SIZE)
    key_raw = projected[:, query_cols : query_cols + kv_cols].reshape(group_rows, kv_dev, HEAD_SIZE)
    value_low = (
        projected[:, query_cols + kv_cols :]
        .astype(jnp.bfloat16)
        .reshape(seq_count, sequence_length, kv_dev, HEAD_SIZE)
    )
    query_factor = inv_root(query_raw)
    key_factor = inv_root(key_raw)
    cosine, sine_tab = rope_tables(sequence_length, HEAD_SIZE)
    cos_rows = jnp.tile(cosine, (seq_count, 1))[:, None, :]
    sin_rows = jnp.tile(sine_tab, (seq_count, 1))[:, None, :]
    query_low = (
        rotate(query_raw * query_factor * query_gain, cos_rows, sin_rows)
        .astype(jnp.bfloat16)
        .reshape(seq_count, sequence_length, heads_dev, HEAD_SIZE)
    )
    key_low = (
        rotate(key_raw * key_factor * key_gain, cos_rows, sin_rows)
        .astype(jnp.bfloat16)
        .reshape(seq_count, sequence_length, kv_dev, HEAD_SIZE)
    )
    attended, summit = lax.map(
        lambda packed: attend(packed[0], packed[1], packed[2], packed[3], kv_dev),
        (query_low, key_low, value_low, prefix),
    )
    attended_low = attended.reshape(group_rows, query_cols).astype(jnp.bfloat16)
    middle = source + lax.psum_scatter(
        jnp.dot(attended_low, w_out, preferred_element_type=jnp.float32),
        "tensor",
        scatter_dimension=0,
        tiled=True,
    )
    factor_two = inv_root(middle)
    normed_two = (middle * factor_two * ffn_gain).astype(jnp.bfloat16)
    normed_two_all = lax.all_gather(normed_two, "tensor", axis=0, tiled=True)
    gate_act = jnp.dot(normed_two_all, w_gate, preferred_element_type=jnp.float32)
    up_act = jnp.dot(normed_two_all, w_up, preferred_element_type=jnp.float32)
    sig_gate = jax.nn.sigmoid(gate_act)
    hidden = (gate_act * sig_gate * up_act).astype(jnp.bfloat16)
    result = middle + lax.psum_scatter(
        jnp.dot(hidden, w_down, preferred_element_type=jnp.float32).astype(jnp.bfloat16),
        "tensor",
        scatter_dimension=0,
        tiled=True,
    ).astype(jnp.float32)
    mask_rows = valid.astype(jnp.float32)[:, None]
    error_rows = result - teacher.astype(jnp.float32)
    total_count, total_square = lax.psum(
        (jnp.sum(valid).astype(jnp.float32), jnp.sum(error_rows * error_rows * mask_rows)),
        ("dp", "tensor"),
    )
    loss = total_square / (total_count * width)
    cotangent = group_rows * lax.axis_size("dp") / total_count * error_rows * mask_rows
    cot_all = lax.all_gather(cotangent.astype(jnp.bfloat16), "tensor", axis=0, tiled=True)
    grad_down = jnp.einsum("tf,td->fd", hidden, cot_all, preferred_element_type=jnp.float32)
    grad_hidden = jnp.einsum("td,fd->tf", cot_all, w_down, preferred_element_type=jnp.float32)
    grad_gate_low = (grad_hidden * up_act * sig_gate * (1.0 + gate_act * (1.0 - sig_gate))).astype(
        jnp.bfloat16
    )
    grad_up_low = (grad_hidden * gate_act * sig_gate).astype(jnp.bfloat16)
    gate_part = grad_gate_low
    up_part = grad_up_low
    grad_normed_two = lax.psum_scatter(
        (
            jnp.einsum("tf,df->td", gate_part, w_gate, preferred_element_type=jnp.float32)
            + jnp.einsum("tf,df->td", up_part, w_up, preferred_element_type=jnp.float32)
        ).astype(jnp.bfloat16),
        "tensor",
        scatter_dimension=0,
        tiled=True,
    ).astype(jnp.float32)
    grad_ffn_gain = jnp.sum(grad_normed_two * middle * factor_two, 0)
    grad_middle = cotangent + norm_back(grad_normed_two, middle, factor_two, ffn_gain)
    grad_branch_all = lax.all_gather(grad_middle.astype(jnp.bfloat16), "tensor", axis=0, tiled=True)
    grad_out = jnp.einsum(
        "tq,td->qd", attended_low, grad_branch_all, preferred_element_type=jnp.float32
    )
    grad_attended = jnp.einsum(
        "td,qd->tq", grad_branch_all, w_out, preferred_element_type=jnp.float32
    ).astype(jnp.bfloat16)
    grad_q_rot, grad_k_rot, grad_v = lax.map(
        lambda packed: attend_back(
            packed[0], packed[1], packed[2], packed[3], packed[4], packed[5], kv_dev
        ),
        (
            query_low,
            key_low,
            value_low,
            prefix,
            summit,
            grad_attended.reshape(seq_count, sequence_length, query_cols),
        ),
    )
    grad_k_rot = grad_k_rot.reshape(group_rows, kv_dev, HEAD_SIZE)
    grad_v = grad_v.reshape(group_rows, kv_cols)
    grad_q_normed = unrotate(
        grad_q_rot.reshape(group_rows, heads_dev, HEAD_SIZE), cos_rows, sin_rows
    )
    grad_k_normed = unrotate(grad_k_rot, cos_rows, sin_rows)
    grad_query_gain = jnp.sum(grad_q_normed * query_raw * query_factor, (0, 1))
    grad_key_gain = jnp.sum(grad_k_normed * key_raw * key_factor, (0, 1))
    grad_q_raw = norm_back(grad_q_normed, query_raw, query_factor, query_gain)
    grad_k_raw = norm_back(grad_k_normed, key_raw, key_factor, key_gain)
    back_rows = jnp.concatenate(
        [
            grad_q_raw.reshape(group_rows, query_cols),
            grad_k_raw.reshape(group_rows, kv_cols),
            grad_v,
        ],
        1,
    ).astype(jnp.bfloat16)
    grad_normed = lax.psum_scatter(
        jnp.einsum("tc,dc->td", back_rows, proj_weight, preferred_element_type=jnp.float32).astype(
            jnp.bfloat16
        ),
        "tensor",
        scatter_dimension=0,
        tiled=True,
    ).astype(jnp.float32)
    grad_attn_gain = jnp.sum(grad_normed * source * factor_one, 0)
    grad_tokens = grad_middle + norm_back(grad_normed, source, factor_one, attn_gain)
    grad_proj = jnp.einsum(
        "td,tc->dc",
        lax.all_gather(normed_input, "tensor", axis=0, tiled=True),
        back_rows,
        preferred_element_type=jnp.float32,
    )
    shard_rows = lax.all_gather(normed_two, "tensor", axis=0, tiled=True)
    gate_part = grad_gate_low
    up_part = grad_up_low
    grad_gate = jnp.einsum("td,tf->df", shard_rows, gate_part, preferred_element_type=jnp.float32)
    grad_up = jnp.einsum("td,tf->df", shard_rows, up_part, preferred_element_type=jnp.float32)
    grad_query = grad_proj[:, :query_cols]
    zero_kv = jnp.zeros((width, key_weight.shape[1]), jnp.float32)
    key_full = lax.dynamic_update_slice_in_dim(
        zero_kv, grad_proj[:, query_cols : query_cols + kv_cols], kv_start, 1
    )
    value_full = lax.dynamic_update_slice_in_dim(
        zero_kv, grad_proj[:, query_cols + kv_cols :], kv_start, 1
    )
    grad_query, grad_out, grad_gate, grad_up, grad_down = (
        lax.psum(grad_query.astype(jnp.bfloat16), "dp").astype(jnp.float32),
        lax.psum(grad_out.astype(jnp.bfloat16), "dp").astype(jnp.float32),
        lax.psum(grad_gate.astype(jnp.bfloat16), "dp").astype(jnp.float32),
        lax.psum(grad_up.astype(jnp.bfloat16), "dp").astype(jnp.float32),
        lax.psum(grad_down.astype(jnp.bfloat16), "dp").astype(jnp.float32),
    )
    key_full, value_full, grad_query_gain, grad_key_gain, grad_attn_gain, grad_ffn_gain = lax.psum(
        (key_full, value_full, grad_query_gain, grad_key_gain, grad_attn_gain, grad_ffn_gain),
        ("dp", "tensor"),
    )
    return (
        result.astype(jnp.bfloat16),
        loss,
        grad_tokens,
        grad_query,
        key_full,
        value_full,
        grad_query_gain,
        grad_key_gain,
        grad_out,
        grad_attn_gain,
        grad_ffn_gain,
        grad_gate,
        grad_up,
        grad_down,
    )


def solution(mesh):
    placed = (
        P(("dp", "tensor"), None),
        P(("dp", "tensor"), None),
        P(("dp", "tensor")),
        P("dp"),
        P(None, "tensor"),
        P(),
        P(),
        P(),
        P(),
        P("tensor", None),
        P(),
        P(),
        P(None, "tensor"),
        P(None, "tensor"),
        P("tensor", None),
    )
    return jax.shard_map(
        body,
        mesh=mesh,
        in_specs=placed,
        out_specs=(
            P(("dp", "tensor"), None),
            P(),
            P(("dp", "tensor"), None),
            P(None, "tensor"),
            P(),
            P(),
            P(),
            P(),
            P("tensor", None),
            P(),
            P(),
            P(None, "tensor"),
            P(None, "tensor"),
            P("tensor", None),
        ),
        check_vma=False,
    )
```

profile of v0, /device:TPU:0, one launch (start us, length us, event | category | flops | bytes accessed | tf_op | source)
XLA Modules:
  0.0 2096.8 jit_solution(9297197625935668544)
XLA Ops:
  10.5 3.5 fusion.64
  17.7 148.8 %all-gather.5.cloned.1.call-done = bf16[2048,2048]{1,0:T(8,128)(2,1)} async-done(((bf16[512,2048]{1,0:T(8,128)(2,1)}), bf16[2048,2048]{1,0:T(8,128)(2,1)}) %all-gather.5.cloned.1.call-update) | async-done | bytes 8388624 | tf_op jit(solution)/shard_map/all_gather | solution.py:140
  166.5 7.3 fusion.80
  183.8 3.1 concatenate.48
  186.9 3.1 concatenate.49
  192.7 3.7 fusion.75
  196.8 34.9 %while.26 = (s32[]{:T(128)}, bf16[2,1024,256]{2,1,0:T(8,128)(2,1)}, f32[2,1,4,1024]{3,2,1,0:T(4,128)}, bf16[2,1024,1,64]{1,3,2,0:T(8,128)(2,1)S(1)}, s32[2]{0:T(...) while((s32[]{:T(128)}, bf16[2,1024,256]{2,1,0:T(8,128)(2,1)}, ...), condition=%wide.region_6.7_spmd, body=%wide.region_3.6_spmd.sunk | while | flops 1135604736 | bytes 58068088 | solution.py:165
  199.1 3.9 fusion.150
  203.0 4.2 fusion.151
  207.2 5.6 fusion.152
  216.3 3.9 fusion.150
  220.2 4.2 fusion.151
  224.4 5.6 fusion.152
  231.7 9.8 fusion.93
  241.6 278.6 %reduce-scatter.5.cloned.1.call-done = f32[512,2048]{1,0:T(8,128)} async-done(((f32[2048,2048]{1,0:T(8,128)}), f32[512,2048]{1,0:T(8,128)}) %reduce-scatter.5.cloned.1.call-update) | async-done | bytes 4194320 | tf_op jit(solution)/shard_map/reduce_scatter | solution.py:170
  520.3 4.7 multiply_reduce_fusion.1
  526.2 3.9 multiply_convert_fusion.3
  530.1 150.5 %all-gather.7.cloned.1.call-done = bf16[2048,2048]{1,0:T(8,128)(2,1)} async-done(((bf16[512,2048]{1,0:T(8,128)(2,1)}), bf16[2048,2048]{1,0:T(8,128)(2,1)}) %all-gather.7.cloned.1.call-update) | async-done | bytes 8388624 | tf_op jit(solution)/shard_map/all_gather | solution.py:178
  680.6 16.8 fusion.94
  697.5 17.2 multiply_convert_fusion.2
  714.7 16.6 convolution_convert_fusion.1
  733.2 43.1 %psum.92 = f32[]{:T(128)} all-reduce(f32[]{:T(128)S(6)} %convert_element_type.123), channel_id=1, replica_groups=mesh['dp'=8,'tensor'=4] {'dp','tensor'}, use_global_device_ids=true, to_apply=%region_13.14 | all-reduce | flops 1 | bytes 8 | tf_op jit(solution)/shard_map/psum | solution.py:191
  777.0 98.1 %reduce-scatter.7.cloned.1.call-done = bf16[512,2048]{1,0:T(8,128)(2,1)} async-done(((bf16[2048,2048]{1,0:T(8,128)(2,1)}), bf16[512,2048]{1,0:T(8,128)(2,1)}) %reduce-scatter.7.cloned.1.call-update) | async-done | bytes 2097168 | tf_op jit(solution)/shard_map/reduce_scatter | solution.py:183
  875.1 5.4 fusion.69
  880.6 150.5 %all-gather.9.cloned.1.call-done = bf16[2048,2048]{1,0:T(8,128)(2,1)} async-done(((bf16[512,2048]{1,0:T(8,128)(2,1)}), bf16[2048,2048]{1,0:T(8,128)(2,1)}) %all-gather.9.cloned.1.call-update) | async-done | bytes 8388624 | tf_op jit(solution)/shard_map/all_gather | solution.py:197
  1031.1 24.3 %multiply_convert_fusion = (bf16[2048,1280]{1,0:T(8,128)(2,1)}, bf16[2048,1280]{1,0:T(8,128)(2,1)}) fusion(f32[2048,1280]{1,0:T(8,128)} %fusion.94, f32[2048,1280]{1,0:T(8,128)} %get-tuple-element.296, bf16[2048,2048]{1,0:T(8,128)(2,1)} %all-gather.9.cloned.1.call-done, bf16[1280,2048]{1,0:T(8,128)(2,1)} %param.33), kind=kOutput, calls=%fused_computation.65 | convolution fusion | flops 10771496960 | bytes 45088768 | tf_op jit(solution)/shard_map/td,fd->tf/dot_general | solution.py:199
  1055.4 17.9 fusion.95
  1073.3 19.4 add_convert_fusion
  1092.8 142.8 %reduce-scatter.9.cloned.1.call-done = bf16[512,2048]{1,0:T(8,128)(2,1)} async-done(((bf16[2048,2048]{1,0:T(8,128)(2,1)}), bf16[512,2048]{1,0:T(8,128)(2,1)}) %reduce-scatter.9.cloned.1.call-update) | async-done | bytes 2097168 | tf_op jit(solution)/shard_map/reduce_scatter | solution.py:206
  1235.6 5.8 fusion.61
  1241.4 6.3 fusion.88
  1250.9 16.9 convolution_convert_fusion.2
  1267.8 15.5 convolution_convert_fusion.3
  1283.4 13.7 convolution_convert_fusion.4
  1297.1 101.2 %all-gather.11.cloned.1.call-done = bf16[2048,2048]{1,0:T(8,128)(2,1)} async-done(((bf16[512,2048]{1,0:T(8,128)(2,1)}), bf16[2048,2048]{1,0:T(8,128)(2,1)}) %all-gather.11.cloned.1.call-update) | async-done | bytes 8388624 | tf_op jit(solution)/shard_map/all_gather | solution.py:217
  1398.3 6.7 convolution_convert_fusion.6
  1405.0 125.9 %while.27 = (s32[]{:T(128)}, f32[2,1024,4,64]{1,0,3,2:T(2,128)}, f32[2,1024,1,64]{1,0,3,2:T(2,128)}, bf16[2,1024,1,64]{1,3,2,0:T(8,128)(2,1)}, bf16[2,1024,1,64]...) while((s32[]{:T(128)}, f32[2,1024,4,64]{1,0,3,2:T(2,128)}, ...), condition=%wide.region_18.19_spmd, body=%wide.region_16.18_spmd.sunk | while | flops 2729767936 | bytes 147803392 | solution.py:224
  1409.9 3.3 fusion.161
  1413.2 10.5 fusion.163
  1423.7 9.1 fusion.167
  1432.8 8.0 fusion.164
  1449.3 18.9 dynamic_update_slice.38
  1472.6 3.3 fusion.161
  1475.9 10.5 fusion.163
  1486.4 9.1 fusion.167
  1495.5 8.0 fusion.164
  1511.9 18.9 dynamic_update_slice.38
  1539.1 3.1 reshape.393
  1548.7 3.5 fusion.76
  1555.0 3.3 convolution_convert_fusion.5
  1559.5 9.3 convolution_convert_fusion
  1573.3 5.8 dynamic_update_slice.26
  1579.2 8.7 dynamic_update_slice.25
  1590.0 197.7 %all-reduce.8.cloned.1.call-done = (bf16[2048,256]{0,1:T(8,128)(2,1)}, bf16[256,2048]{1,0:T(8,128)(2,1)}, bf16[2048,1280]{1,0:T(8,128)(2,1)}, bf16[2048,1280]{1,0:T(8,128)(2,1)}, bf16[1280,2048]{1,0:T(8,128)(2,1)}) async-done(((bf16[2048,256]{0,1:T(8,128)(2,1)}, bf16[256,2048]{1,0:T(8,128)(2,1)}, bf16[2048,1280]{1,0:T(8,128)(2,1)}, bf16[2048,1280]{1,0:T(8,128)(2,1)}, bf16[1280,2048]{1,0:T(8,128)(2,1)}), ...) | async-done | bytes 17825808 | tf_op jit(solution)/shard_map/psum | solution.py:285
  1790.3 2.9 convert_element_type.135
  1793.3 7.5 convert_element_type.137
  1800.8 4.9 convert_element_type.139
  1805.7 5.5 convert_element_type.141
  1811.2 123.4 %reduce-scatter.11.cloned.1.call-done = bf16[512,2048]{1,0:T(8,128)(2,1)} async-done(((bf16[2048,2048]{1,0:T(8,128)(2,1)}), bf16[512,2048]{1,0:T(8,128)(2,1)}) %reduce-scatter.11.cloned.1.call-update) | async-done | bytes 2097168 | tf_op jit(solution)/shard_map/reduce_scatter | solution.py:255
  1934.7 3.2 fusion.68
  1937.8 41.8 %all-reduce = (f32[]{:T(128)}, f32[64]{0:T(128)}, f32[64]{0:T(128)}, f32[2048]{0:T(1024)}, f32[2048]{0:T(1024)}) all-reduce(f32[]{:T(128)} %get-tuple-element.206, f32[64]{0:T(128)S(1)} %reduce_sum.163, f32[64]{0:T(128)S(1)} %get-tuple-element.209, ...), channel_id=1, replica_groups=mesh['dp'=8,'tensor'=4] {'dp','tensor'}, use_global_device_ids=true, to_apply=%region_11.12 | all-reduce | flops 4225 | bytes 33800 | tf_op jit(solution)/shard_map/psum | solution.py:191
  1980.3 6.1 fusion.56
  1986.4 97.6 %all-reduce.6.cloned.1.call-done = (f32[2048,256]{1,0:T(8,128)}, f32[2048,256]{1,0:T(8,128)}) async-done(((f32[2048,256]{1,0:T(8,128)}, f32[2048,256]{1,0:T(8,128)}), (f32[2048,256]{1,0:T(8,128)}, f32[2048,256]{1,0:T(8,128)})) %all-reduce.6.cloned.1.call-update) | async-done | bytes 4194320 | tf_op jit(solution)/shard_map/psum | solution.py:291
  2084.0 3.2 copy.160
  (275 shorter events, 86.9 us)
Async XLA Ops:
  7.2 224.5 %copy-start = (bf16[256,2048]{1,0:T(8,128)(2,1)S(1)}, bf16[256,2048]{1,0:T(8,128)(2,1)}, u32[]{:S(2)}) copy-start(bf16[256,2048]{1,0:T(8,128)(2,1)} %param.28) | copy-start | bytes 3145732
  7.2 159.3 %all-gather.5.cloned.1.call-start = ((), (), s32[]{:S(2)}) async-start(), calls=%async_computation.4 | async-start | bytes 10485760 | tf_op jit(solution)/shard_map/all_gather | solution.py:140
  14.0 506.2 %reduce-scatter.5.cloned.1.call-start = ((), (), s32[]{:S(2)}) async-start(), calls=%async_computation.5 | async-start | bytes 20971520 | tf_op jit(solution)/shard_map/reduce_scatter | solution.py:170
  15.1 163.1 %copy-start.16 = (f32[8,8,2,1024]{3,1,2,0:T(8,128)}, f32[8,8,2,1024]{3,1,2,0:T(8,128)S(1)}, u32[]{:S(2)}) copy-start(f32[8,8,2,1024]{3,1,2,0:T(8,128)S(1)} %copy.112) | copy-start | bytes 1572868
  15.9 162.3 %copy-start.7 = (f32[8,8,2,1024]{3,1,2,0:T(8,128)}, f32[8,8,2,1024]{3,1,2,0:T(8,128)S(1)}, u32[]{:S(2)}) copy-start(f32[8,8,2,1024]{3,1,2,0:T(8,128)S(1)} %copy.111) | copy-start | bytes 1572868
  17.7 156.1 %copy-start.28 = (bf16[2048,64]{1,0:T(8,128)(2,1)}, bf16[2048,64]{1,0:T(8,128)(2,1)S(1)}, u32[]{:S(2)}) copy-start(bf16[2048,64]{1,0:T(8,128)(2,1)S(1)} %get-tuple-element.297) | copy-start | bytes 786436
  17.7 156.1 %copy-start.30 = (bf16[2048,64]{1,0:T(8,128)(2,1)}, bf16[2048,64]{1,0:T(8,128)(2,1)S(1)}, u32[]{:S(2)}) copy-start(bf16[2048,64]{1,0:T(8,128)(2,1)S(1)} %get-tuple-element.298) | copy-start | bytes 786436
  173.8 3.2 copy-start.49
  175.5 4.9 copy-start.45
  176.1 6.2 copy-start.33
  176.7 5.6 copy-start.26
  182.3 7.6 slice-start
  192.7 4.0 copy-start.55
  231.7 9.8 copy-start.10
  231.7 9.9 copy-start.18
  241.5 278.7 %copy-start.3 = (bf16[512,2048]{1,0:T(8,128)(2,1)S(1)}, bf16[512,2048]{1,0:T(8,128)(2,1)}, u32[]{:S(2)}) copy-start(bf16[512,2048]{1,0:T(8,128)(2,1)} %param.19) | copy-start | bytes 6291460
  241.6 284.6 %copy-start.36 = (f32[2048]{0:T(1024)S(1)}, f32[2048]{0:T(1024)}, u32[]{:S(2)}) copy-start(f32[2048]{0:T(1024)} %param.30) | copy-start | bytes 24580
  241.6 439.1 %all-gather.7.cloned.1.call-start = ((), (), s32[]{:S(2)}) async-start(), calls=%async_computation.6 | async-start | bytes 10485760 | tf_op jit(solution)/shard_map/all_gather | solution.py:178
  530.1 345.0 %reduce-scatter.7.cloned.1.call-start = ((), (), s32[]{:S(2)}) async-start(), calls=%async_computation.7 | async-start | bytes 10485760 | tf_op jit(solution)/shard_map/reduce_scatter | solution.py:183
  680.6 16.8 copy-start.54
  731.2 143.9 %copy-start.5 = (bf16[512,2048]{1,0:T(8,128)(2,1)S(1)}, bf16[512,2048]{1,0:T(8,128)(2,1)}, u32[]{:S(2)}) copy-start(bf16[512,2048]{1,0:T(8,128)(2,1)} %param.20) | copy-start | bytes 6291460
  731.3 299.8 %all-gather.9.cloned.1.call-start = ((), (), s32[]{:S(2)}) async-start(), calls=%async_computation.8 | async-start | bytes 10485760 | tf_op jit(solution)/shard_map/all_gather | solution.py:197
  880.6 355.0 %reduce-scatter.9.cloned.1.call-start = ((), (), s32[]{:S(2)}) async-start(), calls=%async_computation.9 | async-start | bytes 10485760 | tf_op jit(solution)/shard_map/reduce_scatter | solution.py:206
  1092.7 142.9 %copy-start.37 = (f32[2048]{0:T(1024)S(1)}, f32[2048]{0:T(1024)}, u32[]{:S(2)}) copy-start(f32[2048]{0:T(1024)} %param.30) | copy-start | bytes 24580
  1092.7 142.9 %copy-start.44 = (f32[512]{0:T(512)S(1)}, f32[512]{0:T(512)}, u32[]{:S(2)}) copy-start(f32[512]{0:T(512)} %copy-done.43) | copy-start | bytes 6148
  1092.7 148.7 %copy-start.48 = (f32[512]{0:T(512)S(1)}, f32[512]{0:T(512)}, u32[]{:S(2)}) copy-start(f32[512]{0:T(512)} %get-tuple-element.289) | copy-start | bytes 6148
  1092.7 305.6 %all-gather.11.cloned.1.call-start = ((), (), s32[]{:S(2)}) async-start(), calls=%async_computation.10 | async-start | bytes 10485760 | tf_op jit(solution)/shard_map/all_gather | solution.py:217
  1235.6 5.8 copy-start.6
  1235.6 5.8 copy-start.12
  1241.4 8.8 copy-start.46
  1247.8 20.1 slice-start.13
  1247.8 540.0 %all-reduce.8.cloned.1.call-start = ((), (), s32[]{:S(2)}) async-start(), calls=%async_computation.13 | async-start | bytes 35651584 | tf_op jit(solution)/shard_map/psum | solution.py:285
  1250.9 16.9 slice-start.14
  1250.9 32.5 %slice-start.9 = ((s8[8388608]{0:T(1024)(128)(4,1)}), s8[4194304]{0:T(1024)(128)(4,1)S(1)}, s32[]{:S(2)}) async-start(s8[8388608]{0:T(1024)(128)(4,1)} %bitcast.333), calls=%async_computation.23 | async-start | bytes 8388608
  1250.9 32.5 %slice-start.11 = ((s8[5242880]{0:T(1024)(128)(4,1)}), s8[4194304]{0:T(1024)(128)(4,1)S(1)}, s32[]{:S(2)}) async-start(s8[5242880]{0:T(1024)(128)(4,1)} %bitcast.335), calls=%async_computation.25 | async-start | bytes 8388608
  1267.8 15.5 slice-start.10
  1267.8 15.5 slice-start.12
  1297.1 108.0 %copy-start.56 = (s32[2]{0:T(128)S(1)}, s32[2]{0:T(128)}, u32[]{:S(2)}) copy-start(s32[2]{0:T(128)} %param.22) | copy-start | bytes 28
  1432.8 8.0 copy-start.11
  1443.4 3.9 copy-start.23
  1449.2 18.9 copy-start.24
  1495.4 8.0 copy-start.11
  1506.1 3.9 copy-start.23
  1511.9 18.9 copy-start.24
  1531.0 5.9 copy-start.8
  1531.0 5.9 copy-start.34
  1531.0 5.9 copy-start.50
  1544.3 3.7 slice-start.7
  1545.9 2.8 slice-start.8
  1547.0 8.0 slice-start.1
  1548.7 6.3 slice-start.2
  1548.7 6.3 copy-start.15
  1558.4 376.3 %reduce-scatter.11.cloned.1.call-start = ((), (), s32[]{:S(2)}) async-start(), calls=%async_computation.11 | async-start | bytes 10485760 | tf_op jit(solution)/shard_map/reduce_scatter | solution.py:255
  1568.8 515.2 %all-reduce.6.cloned.1.call-start = ((), (), s32[]{:S(2)}) async-start(), calls=%async_computation.12 | async-start | bytes 8388608 | tf_op jit(solution)/shard_map/psum | solution.py:291
  1790.3 10.5 slice-start.5
  1793.3 7.5 slice-start.6
  1793.3 12.4 slice-start.3
  1800.8 4.9 slice-start.4
  1805.7 128.9 %copy-start.4 = (bf16[512,2048]{1,0:T(8,128)(2,1)S(1)}, bf16[512,2048]{1,0:T(8,128)(2,1)}, u32[]{:S(2)}) copy-start(bf16[512,2048]{1,0:T(8,128)(2,1)} %param.19) | copy-start | bytes 6291460
  1805.7 128.9 %copy-start.38 = (f32[2048]{0:T(1024)S(1)}, f32[2048]{0:T(1024)}, u32[]{:S(2)}) copy-start(f32[2048]{0:T(1024)} %param.29) | copy-start | bytes 24580
  1805.7 128.9 %copy-start.41 = (f32[512]{0:T(512)S(1)}, f32[512]{0:T(512)}, u32[]{:S(2)}) copy-start(f32[512]{0:T(512)} %copy-done.40) | copy-start | bytes 6148
  1811.2 126.6 %copy-start.42 = (f32[2048]{0:T(1024)S(1)}, f32[2048]{0:T(1024)}, u32[]{:S(2)}) copy-start(f32[2048]{0:T(1024)} %get-tuple-element.204) | copy-start | bytes 24580
  1811.2 169.1 %copy-start.51 = (f32[512]{0:T(512)S(1)}, f32[512]{0:T(512)}, u32[]{:S(2)}) copy-start(f32[512]{0:T(512)} %get-tuple-element.287) | copy-start | bytes 6148
  2084.0 3.2 copy-start.22
  (21 other events, 29.7 us)
Sparse Core Ops, SparseCore 0:
  14.1 152.3 all-gather.4
  241.7 278.5 reduce-scatter.4
  530.2 150.3 all-gather.6
  731.4 143.6 reduce-scatter.6
  880.7 150.3 all-gather.8
  1092.8 142.6 reduce-scatter.8
  1247.9 150.3 all-gather.10
  1558.5 229.2 all-reduce.7
  1790.1 144.4 reduce-scatter.10
  1940.8 143.1 all-reduce.5
where the time goes:
time: 2110 us; the launch traced here: 2100 us
  waiting for transfers between devices  1490 us (71%)
  matrix products  273 us (13%)
  local copies, waits for them, and re-layouts  115 us (5%)
  other arithmetic  113 us (5%)
  blocking collectives  84.9 us (4%)
    reduce_scatter x1, waiting for transfers between devices, body(): lax.psum_scatter(jnp.dot(attended_low, w_out, preferred_element_type=jnp....  279 us
    psum x1, waiting for transfers between devices, body(): lax.psum(grad_query.astype(jnp.bfloat16), 'dp').astype(jnp.float32)  198 us
    all_gather x1, waiting for transfers between devices, body(): normed_two_all = lax.all_gather(normed_two, 'tensor', axis=0, tiled=True)  150 us
    all_gather x1, waiting for transfers between devices, body(): lax.all_gather(cotangent.astype(jnp.bfloat16), 'tensor', axis=0, tiled=True)  150 us
    all_gather x1, waiting for transfers between devices, body(): normed_all = lax.all_gather(normed_input, 'tensor', axis=0, tiled=True)  149 us
    reduce_scatter x1, waiting for transfers between devices, body(): lax.psum_scatter((jnp.einsum('tf,df->td', gate_part, w_gate, preferred_el...  143 us
    reduce_scatter x1, waiting for transfers between devices, body(): lax.psum_scatter(jnp.einsum('tc,dc->td', back_rows, proj_weight, preferre...  123 us
    all_gather x1, waiting for transfers between devices, body(): lax.all_gather(grad_middle.astype(jnp.bfloat16), 'tensor', axis=0, tiled=...  101 us
  transfers between devices with their start and end apart: 10, of which 10 were waited for; matrix products, arithmetic and copies ran while one was open for 5% of the time, Pallas kernels for 0%

commit v1 on v0

--- a/solution.py
+++ b/solution.py
@@ -282,7 +282,9 @@
         zero_kv, grad_proj[:, query_cols + kv_cols :], kv_start, 1
     )
     grad_query, grad_out, grad_gate, grad_up, grad_down = (
-        lax.psum(grad_query.astype(jnp.bfloat16), "dp").astype(jnp.float32),
+        jnp.sum(jax.lax.all_gather(grad_query.astype(jnp.bfloat16), "dp"), axis=0).astype(
+            jnp.float32
+        ),
         lax.psum(grad_out.astype(jnp.bfloat16), "dp").astype(jnp.float32),
         lax.psum(grad_gate.astype(jnp.bfloat16), "dp").astype(jnp.float32),
         lax.psum(grad_up.astype(jnp.bfloat16), "dp").astype(jnp.float32),

time: 2110 us -> 2000 us (0.948)
  waiting for transfers between devices: 1490 us -> 1350 us
    psum x1, waiting for transfers between devices: 198 us -> 26.6 us  [body(): lax.psum(grad_out.astype(jnp.bfloat16), 'dp').astype(jnp.float32)]
    all_gather x0 -> x1, waiting for transfers between devices: none -> 35.9 us  [body(): jax.lax.all_gather(grad_query.astype(jnp.bfloat16), 'dp')]
  transfers between devices with their start and end apart: 10 -> 11, of which waited for: 10 -> 11; matrix products, arithmetic and copies ran while one was open for 5% -> 15% of each run, Pallas kernels for 0% -> 0%
where the time goes in v1:
time: 2000 us; the launch traced here: 1990 us
  waiting for transfers between devices  1350 us (68%)
  matrix products  279 us (14%)
  local copies, waits for them, and re-layouts  136 us (7%)
  other arithmetic  121 us (6%)
  blocking collectives  85 us (4%)
    reduce_scatter x1, waiting for transfers between devices, body(): lax.psum_scatter(jnp.dot(attended_low, w_out, preferred_element_type=jnp....  279 us
    all_gather x1, waiting for transfers between devices, body(): normed_two_all = lax.all_gather(normed_two, 'tensor', axis=0, tiled=True)  150 us
    all_gather x1, waiting for transfers between devices, body(): lax.all_gather(cotangent.astype(jnp.bfloat16), 'tensor', axis=0, tiled=True)  150 us
    all_gather x1, waiting for transfers between devices, body(): normed_all = lax.all_gather(normed_input, 'tensor', axis=0, tiled=True)  149 us
    reduce_scatter x1, waiting for transfers between devices, body(): lax.psum_scatter((jnp.einsum('tf,df->td', gate_part, w_gate, preferred_el...  143 us
    reduce_scatter x1, waiting for transfers between devices, body(): lax.psum_scatter(jnp.einsum('tc,dc->td', back_rows, proj_weight, preferre...  116 us
    all_gather x1, waiting for transfers between devices, body(): lax.all_gather(grad_middle.astype(jnp.bfloat16), 'tensor', axis=0, tiled=...  101 us
    reduce_scatter x1, waiting for transfers between devices, body(): lax.psum_scatter(jnp.dot(hidden, w_down, preferred_element_type=jnp.float...  98.1 us
  transfers between devices with their start and end apart: 11, of which 11 were waited for; matrix products, arithmetic and copies ran while one was open for 15% of the time, Pallas kernels for 0%

profile of v1, /device:TPU:0, one launch (start us, length us, event | category | flops | bytes accessed | tf_op | source)
XLA Modules:
  0.0 1988.1 jit_solution(3349286924488627420)
XLA Ops:
  10.6 3.5 fusion.64
  17.7 148.8 %all-gather.7.cloned.1.call-done = bf16[2048,2048]{1,0:T(8,128)(2,1)} async-done(((bf16[512,2048]{1,0:T(8,128)(2,1)}), bf16[2048,2048]{1,0:T(8,128)(2,1)}) %all-gather.7.cloned.1.call-update) | async-done | bytes 8388624 | tf_op jit(solution)/shard_map/all_gather | solution.py:140
  166.5 7.3 fusion.80
  183.8 3.1 concatenate.48
  192.7 3.7 fusion.75
  196.8 34.9 %while.26 = (s32[]{:T(128)}, bf16[2,1024,256]{2,1,0:T(8,128)(2,1)}, f32[2,1,4,1024]{3,2,1,0:T(4,128)}, bf16[2,1024,1,64]{1,3,2,0:T(8,128)(2,1)S(1)}, s32[2]{0:T(...) while((s32[]{:T(128)}, bf16[2,1024,256]{2,1,0:T(8,128)(2,1)}, ...), condition=%wide.region_6.7_spmd, body=%wide.region_3.6_spmd.sunk | while | flops 1135604736 | bytes 58068088 | solution.py:165
  199.1 3.9 fusion.150
  203.0 4.2 fusion.151
  207.2 5.6 fusion.152
  216.3 3.9 fusion.150
  220.2 4.2 fusion.151
  224.4 5.6 fusion.152
  231.7 9.8 fusion.93
  241.6 278.6 %reduce-scatter.5.cloned.1.call-done = f32[512,2048]{1,0:T(8,128)} async-done(((f32[2048,2048]{1,0:T(8,128)}), f32[512,2048]{1,0:T(8,128)}) %reduce-scatter.5.cloned.1.call-update) | async-done | bytes 4194320 | tf_op jit(solution)/shard_map/reduce_scatter | solution.py:170
  520.2 4.7 multiply_reduce_fusion.1
  526.1 3.9 multiply_convert_fusion.3
  530.1 150.5 %all-gather.9.cloned.1.call-done = bf16[2048,2048]{1,0:T(8,128)(2,1)} async-done(((bf16[512,2048]{1,0:T(8,128)(2,1)}), bf16[2048,2048]{1,0:T(8,128)(2,1)}) %all-gather.9.cloned.1.call-update) | async-done | bytes 8388624 | tf_op jit(solution)/shard_map/all_gather | solution.py:178
  680.6 16.8 fusion.94
  697.5 17.2 multiply_convert_fusion.2
  714.7 16.6 convolution_convert_fusion.1
  733.2 43.1 %psum.85 = f32[]{:T(128)} all-reduce(f32[]{:T(128)S(6)} %convert_element_type.125), channel_id=1, replica_groups=mesh['dp'=8,'tensor'=4] {'dp','tensor'}, use_global_device_ids=true, to_apply=%region_13.14 | all-reduce | flops 1 | bytes 8 | tf_op jit(solution)/shard_map/psum | solution.py:191
  777.0 98.1 %reduce-scatter.7.cloned.1.call-done = bf16[512,2048]{1,0:T(8,128)(2,1)} async-done(((bf16[2048,2048]{1,0:T(8,128)(2,1)}), bf16[512,2048]{1,0:T(8,128)(2,1)}) %reduce-scatter.7.cloned.1.call-update) | async-done | bytes 2097168 | tf_op jit(solution)/shard_map/reduce_scatter | solution.py:183
  875.1 5.4 fusion.69
  880.6 150.5 %all-gather.11.cloned.1.call-done = bf16[2048,2048]{1,0:T(8,128)(2,1)} async-done(((bf16[512,2048]{1,0:T(8,128)(2,1)}), bf16[2048,2048]{1,0:T(8,128)(2,1)}) %all-gather.11.cloned.1.call-update) | async-done | bytes 8388624 | tf_op jit(solution)/shard_map/all_gather | solution.py:197
  1031.1 24.3 %multiply_convert_fusion = (bf16[2048,1280]{1,0:T(8,128)(2,1)}, bf16[2048,1280]{1,0:T(8,128)(2,1)}) fusion(f32[2048,1280]{1,0:T(8,128)} %fusion.94, f32[2048,1280]{1,0:T(8,128)} %get-tuple-element.298, bf16[2048,2048]{1,0:T(8,128)(2,1)} %all-gather.11.cloned.1.call-done, bf16[1280,2048]{1,0:T(8,128)(2,1)} %param.33), kind=kOutput, calls=%fused_computation.65 | convolution fusion | flops 10771496960 | bytes 45088768 | tf_op jit(solution)/shard_map/td,fd->tf/dot_general | solution.py:199
  1055.3 17.8 fusion.95
  1073.2 19.4 add_convert_fusion
  1092.7 142.8 %reduce-scatter.9.cloned.1.call-done = bf16[512,2048]{1,0:T(8,128)(2,1)} async-done(((bf16[2048,2048]{1,0:T(8,128)(2,1)}), bf16[512,2048]{1,0:T(8,128)(2,1)}) %reduce-scatter.9.cloned.1.call-update) | async-done | bytes 2097168 | tf_op jit(solution)/shard_map/reduce_scatter | solution.py:206
  1235.5 5.8 fusion.61
  1241.3 6.3 fusion.88
  1250.7 17.0 convolution_convert_fusion.2
  1267.7 15.5 convolution_convert_fusion.3
  1283.3 13.7 convolution_convert_fusion.4
  1296.9 101.2 %all-gather.13.cloned.1.call-done = bf16[2048,2048]{1,0:T(8,128)(2,1)} async-done(((bf16[512,2048]{1,0:T(8,128)(2,1)}), bf16[2048,2048]{1,0:T(8,128)(2,1)}) %all-gather.13.cloned.1.call-update) | async-done | bytes 8388624 | tf_op jit(solution)/shard_map/all_gather | solution.py:217
  1398.1 6.7 convolution_convert_fusion.5
  1404.9 6.7 convolution_convert_fusion.6
  1411.7 128.2 %while.27 = (s32[]{:T(128)}, f32[2,1024,4,64]{1,0,3,2:T(2,128)}, f32[2,1024,1,64]{1,0,3,2:T(2,128)}, bf16[2,1024,1,64]{1,3,2,0:T(8,128)(2,1)}, bf16[2,1024,1,64]...) while((s32[]{:T(128)}, f32[2,1024,4,64]{1,0,3,2:T(2,128)}, ...), condition=%wide.region_18.19_spmd, body=%wide.region_16.18_spmd.sunk | while | flops 2729767936 | bytes 147803392 | solution.py:224
  1416.6 3.3 fusion.161
  1419.9 10.5 fusion.163
  1430.4 10.3 fusion.167
  1440.7 8.2 fusion.164
  1457.4 18.9 dynamic_update_slice.38
  1480.9 3.3 fusion.161
  1484.1 10.5 fusion.163
  1494.6 9.6 fusion.167
  1504.2 8.0 fusion.164
  1520.8 18.9 dynamic_update_slice.38
  1558.5 3.5 fusion.76
  1564.9 9.5 convolution_convert_fusion
  1578.9 5.9 dynamic_update_slice.26
  1584.9 9.1 dynamic_update_slice.25
  1596.1 26.6 %all-reduce.8.cloned.1.call-done = (bf16[256,2048]{1,0:T(8,128)(2,1)}, bf16[2048,1280]{1,0:T(8,128)(2,1)}, bf16[2048,1280]{1,0:T(8,128)(2,1)}, bf16[1280,2048]{1,0:T(8,128)(2,1)}) async-done(((bf16[256,2048]{1,0:T(8,128)(2,1)}, bf16[2048,1280]{1,0:T(8,128)(2,1)}, bf16[2048,1280]{1,0:T(8,128)(2,1)}, bf16[1280,2048]{1,0:T(8,128)(2,1)}), (bf16[256,2048]{1,0:T(8,128)(2,1)}, bf16[2048,1280]{1,0:T(8,128)(2,1)}, ...) | async-done | bytes 16777232 | tf_op jit(solution)/shard_map/psum | solution.py:288
  1625.6 7.6 convert_element_type.139
  1633.3 4.9 convert_element_type.141
  1638.2 5.5 convert_element_type.143
  1643.7 35.9 %all-gather.15.cloned.1.call-done = bf16[16384,256]{0,1:T(8,128)(2,1)} async-done(((bf16[2048,256]{0,1:T(8,128)(2,1)}), bf16[16384,256]{0,1:T(8,128)(2,1)}) %all-gather.15.cloned.1.call-update) | async-done | bytes 8388624 | tf_op jit(solution)/shard_map/all_gather | solution.py:285
  1679.6 16.2 copy.134
  1695.8 11.4 bitcast_reduce_fusion
  1709.8 116.4 %reduce-scatter.11.cloned.1.call-done = bf16[512,2048]{1,0:T(8,128)(2,1)} async-done(((bf16[2048,2048]{1,0:T(8,128)(2,1)}), bf16[512,2048]{1,0:T(8,128)(2,1)}) %reduce-scatter.11.cloned.1.call-update) | async-done | bytes 2097168 | tf_op jit(solution)/shard_map/reduce_scatter | solution.py:255
  1826.3 3.2 fusion.68
  1829.4 41.9 %all-reduce = (f32[]{:T(128)}, f32[64]{0:T(128)}, f32[64]{0:T(128)}, f32[2048]{0:T(1024)}, f32[2048]{0:T(1024)}) all-reduce(f32[]{:T(128)} %get-tuple-element.209, f32[64]{0:T(128)S(1)} %reduce_sum.176, f32[64]{0:T(128)S(1)} %get-tuple-element.212, ...), channel_id=1, replica_groups=mesh['dp'=8,'tensor'=4] {'dp','tensor'}, use_global_device_ids=true, to_apply=%region_11.12 | all-reduce | flops 4225 | bytes 33800 | tf_op jit(solution)/shard_map/psum | solution.py:191
  1872.0 6.2 fusion.56
  1878.2 97.6 %all-reduce.6.cloned.1.call-done = (f32[2048,256]{1,0:T(8,128)}, f32[2048,256]{1,0:T(8,128)}) async-done(((f32[2048,256]{1,0:T(8,128)}, f32[2048,256]{1,0:T(8,128)}), (f32[2048,256]{1,0:T(8,128)}, f32[2048,256]{1,0:T(8,128)})) %all-reduce.6.cloned.1.call-update) | async-done | bytes 4194320 | tf_op jit(solution)/shard_map/psum | solution.py:293
  1975.8 3.2 copy.178
  (277 shorter events, 95.9 us)
Async XLA Ops:
  7.2 224.5 %copy-start = (bf16[256,2048]{1,0:T(8,128)(2,1)S(1)}, bf16[256,2048]{1,0:T(8,128)(2,1)}, u32[]{:S(2)}) copy-start(bf16[256,2048]{1,0:T(8,128)(2,1)} %param.28) | copy-start | bytes 3145732
  7.2 159.3 %all-gather.7.cloned.1.call-start = ((), (), s32[]{:S(2)}) async-start(), calls=%async_computation.4 | async-start | bytes 10485760 | tf_op jit(solution)/shard_map/all_gather | solution.py:140
  14.0 506.2 %reduce-scatter.5.cloned.1.call-start = ((), (), s32[]{:S(2)}) async-start(), calls=%async_computation.5 | async-start | bytes 20971520 | tf_op jit(solution)/shard_map/reduce_scatter | solution.py:170
  15.1 163.1 %copy-start.14 = (f32[8,8,2,1024]{3,1,2,0:T(8,128)}, f32[8,8,2,1024]{3,1,2,0:T(8,128)S(1)}, u32[]{:S(2)}) copy-start(f32[8,8,2,1024]{3,1,2,0:T(8,128)S(1)} %copy.130) | copy-start | bytes 1572868
  16.0 162.3 %copy-start.7 = (f32[8,8,2,1024]{3,1,2,0:T(8,128)}, f32[8,8,2,1024]{3,1,2,0:T(8,128)S(1)}, u32[]{:S(2)}) copy-start(f32[8,8,2,1024]{3,1,2,0:T(8,128)S(1)} %copy.129) | copy-start | bytes 1572868
  17.7 156.1 %copy-start.29 = (bf16[2048,64]{1,0:T(8,128)(2,1)}, bf16[2048,64]{1,0:T(8,128)(2,1)S(1)}, u32[]{:S(2)}) copy-start(bf16[2048,64]{1,0:T(8,128)(2,1)S(1)} %get-tuple-element.299) | copy-start | bytes 786436
  17.7 156.1 %copy-start.31 = (bf16[2048,64]{1,0:T(8,128)(2,1)}, bf16[2048,64]{1,0:T(8,128)(2,1)S(1)}, u32[]{:S(2)}) copy-start(bf16[2048,64]{1,0:T(8,128)(2,1)S(1)} %get-tuple-element.300) | copy-start | bytes 786436
  173.8 3.2 copy-start.50
  175.5 4.9 copy-start.46
  176.1 6.2 copy-start.34
  176.7 5.6 copy-start.27
  182.3 7.6 slice-start
  192.7 4.0 copy-start.56
  231.7 9.8 copy-start.9
  231.7 9.8 copy-start.17
  241.5 278.7 %copy-start.3 = (bf16[512,2048]{1,0:T(8,128)(2,1)S(1)}, bf16[512,2048]{1,0:T(8,128)(2,1)}, u32[]{:S(2)}) copy-start(bf16[512,2048]{1,0:T(8,128)(2,1)} %param.19) | copy-start | bytes 6291460
  241.5 284.6 %copy-start.37 = (f32[2048]{0:T(1024)S(1)}, f32[2048]{0:T(1024)}, u32[]{:S(2)}) copy-start(f32[2048]{0:T(1024)} %param.30) | copy-start | bytes 24580
  241.6 439.1 %all-gather.9.cloned.1.call-start = ((), (), s32[]{:S(2)}) async-start(), calls=%async_computation.6 | async-start | bytes 10485760 | tf_op jit(solution)/shard_map/all_gather | solution.py:178
  530.1 345.0 %reduce-scatter.7.cloned.1.call-start = ((), (), s32[]{:S(2)}) async-start(), calls=%async_computation.7 | async-start | bytes 10485760 | tf_op jit(solution)/shard_map/reduce_scatter | solution.py:183
  680.6 16.8 copy-start.55
  731.2 143.9 %copy-start.5 = (bf16[512,2048]{1,0:T(8,128)(2,1)S(1)}, bf16[512,2048]{1,0:T(8,128)(2,1)}, u32[]{:S(2)}) copy-start(bf16[512,2048]{1,0:T(8,128)(2,1)} %param.20) | copy-start | bytes 6291460
  731.3 299.8 %all-gather.11.cloned.1.call-start = ((), (), s32[]{:S(2)}) async-start(), calls=%async_computation.8 | async-start | bytes 10485760 | tf_op jit(solution)/shard_map/all_gather | solution.py:197
  880.5 354.9 %reduce-scatter.9.cloned.1.call-start = ((), (), s32[]{:S(2)}) async-start(), calls=%async_computation.9 | async-start | bytes 10485760 | tf_op jit(solution)/shard_map/reduce_scatter | solution.py:206
  1092.6 142.9 %copy-start.38 = (f32[2048]{0:T(1024)S(1)}, f32[2048]{0:T(1024)}, u32[]{:S(2)}) copy-start(f32[2048]{0:T(1024)} %param.30) | copy-start | bytes 24580
  1092.6 142.9 %copy-start.45 = (f32[512]{0:T(512)S(1)}, f32[512]{0:T(512)}, u32[]{:S(2)}) copy-start(f32[512]{0:T(512)} %copy-done.44) | copy-start | bytes 6148
  1092.6 148.7 %copy-start.49 = (f32[512]{0:T(512)S(1)}, f32[512]{0:T(512)}, u32[]{:S(2)}) copy-start(f32[512]{0:T(512)} %get-tuple-element.291) | copy-start | bytes 6148
  1092.6 305.5 %all-gather.13.cloned.1.call-start = ((), (), s32[]{:S(2)}) async-start(), calls=%async_computation.10 | async-start | bytes 10485760 | tf_op jit(solution)/shard_map/all_gather | solution.py:217
  1235.5 5.8 copy-start.6
  1235.5 5.8 copy-start.11
  1241.3 8.8 copy-start.47
  1247.6 20.1 %slice-start.11 = ((s8[5242880]{0:T(1024)(128)(4,1)}), s8[1048576]{0:T(1024)(128)(4,1)S(1)}, s32[]{:S(2)}) async-start(s8[5242880]{0:T(1024)(128)(4,1)} %bitcast.341), calls=%async_computation.26 | async-start | bytes 2097152
  1247.6 375.0 %all-reduce.8.cloned.1.call-start = ((), (), s32[]{:S(2)}) async-start(), calls=%async_computation.14 | async-start | bytes 33554432 | tf_op jit(solution)/shard_map/psum | solution.py:288
  1250.7 17.0 slice-start.12
  1250.7 32.5 %slice-start.7 = ((s8[8388608]{0:T(1024)(128)(4,1)}), s8[4194304]{0:T(1024)(128)(4,1)S(1)}, s32[]{:S(2)}) async-start(s8[8388608]{0:T(1024)(128)(4,1)} %bitcast.337), calls=%async_computation.22 | async-start | bytes 8388608
  1250.7 32.5 %slice-start.9 = ((s8[5242880]{0:T(1024)(128)(4,1)}), s8[4194304]{0:T(1024)(128)(4,1)S(1)}, s32[]{:S(2)}) async-start(s8[5242880]{0:T(1024)(128)(4,1)} %bitcast.339), calls=%async_computation.24 | async-start | bytes 8388608
  1267.7 15.5 slice-start.8
  1267.7 15.5 slice-start.10
  1283.3 114.9 %copy-start.13 = (bf16[2,1024,256]{2,1,0:T(8,128)(2,1)S(1)}, bf16[2,1024,256]{2,1,0:T(8,128)(2,1)}, u32[]{:S(2)}) copy-start(bf16[2,1024,256]{2,1,0:T(8,128)(2,1)} %get-tuple-element.106) | copy-start | bytes 3145732
  1404.8 6.8 copy-start.57
  1404.9 274.7 %all-gather.15.cloned.1.call-start = ((), (), s32[]{:S(2)}) async-start(), calls=%async_computation.12 | async-start | bytes 9437184 | tf_op jit(solution)/shard_map/all_gather | solution.py:285
  1440.7 8.3 copy-start.10
  1451.6 4.0 copy-start.24
  1457.4 18.9 copy-start.25
  1504.2 8.1 copy-start.10
  1514.9 3.9 copy-start.24
  1520.8 18.9 copy-start.25
  1549.2 2.8 copy-start.20
  1549.2 2.8 copy-start.22
  1549.2 2.9 copy-start.15
  1555.4 3.0 slice-start.6
  1558.5 6.4 copy-start.30
  1558.5 6.4 copy-start.32
  1564.8 261.4 %reduce-scatter.11.cloned.1.call-start = ((), (), s32[]{:S(2)}) async-start(), calls=%async_computation.11 | async-start | bytes 10485760 | tf_op jit(solution)/shard_map/reduce_scatter | solution.py:255
  1574.4 401.4 %all-reduce.6.cloned.1.call-start = ((), (), s32[]{:S(2)}) async-start(), calls=%async_computation.13 | async-start | bytes 8388608 | tf_op jit(solution)/shard_map/psum | solution.py:293
  1622.6 10.6 slice-start.3
  1625.6 7.7 slice-start.4
  1625.6 12.6 slice-start.1
  1633.2 4.9 slice-start.2
  1695.8 130.5 %copy-start.4 = (bf16[512,2048]{1,0:T(8,128)(2,1)S(1)}, bf16[512,2048]{1,0:T(8,128)(2,1)}, u32[]{:S(2)}) copy-start(bf16[512,2048]{1,0:T(8,128)(2,1)} %param.19) | copy-start | bytes 6291460
  1695.8 130.5 %copy-start.39 = (f32[2048]{0:T(1024)S(1)}, f32[2048]{0:T(1024)}, u32[]{:S(2)}) copy-start(f32[2048]{0:T(1024)} %param.29) | copy-start | bytes 24580
  1695.8 130.5 %copy-start.42 = (f32[512]{0:T(512)S(1)}, f32[512]{0:T(512)}, u32[]{:S(2)}) copy-start(f32[512]{0:T(512)} %copy-done.41) | copy-start | bytes 6148
  1707.2 122.2 %copy-start.43 = (f32[2048]{0:T(1024)S(1)}, f32[2048]{0:T(1024)}, u32[]{:S(2)}) copy-start(f32[2048]{0:T(1024)} %get-tuple-element.207) | copy-start | bytes 24580
  1707.2 164.8 %copy-start.52 = (f32[512]{0:T(512)S(1)}, f32[512]{0:T(512)}, u32[]{:S(2)}) copy-start(f32[512]{0:T(512)} %get-tuple-element.289) | copy-start | bytes 6148
  1975.8 3.2 copy-start.23
  (21 other events, 29.6 us)
Sparse Core Ops, SparseCore 0:
  14.2 152.3 all-gather.6
  241.7 278.5 reduce-scatter.4
  530.2 150.3 all-gather.8
  731.4 143.6 reduce-scatter.6
  880.7 150.3 all-gather.10
  1092.7 142.6 reduce-scatter.8
  1247.7 150.3 all-gather.12
  1405.0 217.6 all-reduce.7
  1625.1 54.3 all-gather.14
  1681.8 144.4 reduce-scatter.10
  1832.6 143.1 all-reduce.5
